TPU v7x, 256 devices: a whole 4x4x8 slice. The times are simulated.
256 devices in a mesh: dp: 16 (over z, core), blk: 16 (over y, x).
Axes of the slice: x: 4, y: 4, z: 8, core: 2. Of those that a mesh axis runs over, the one named last changes fastest.
Arguments:
- frames: bfloat16 [64, 1280, 256], P('dp', 'blk'), may hold values from -6 to 6
- weight: bfloat16 [1280, 11520], P('blk'), may hold values from -0.0546875 to 0.0546875
- bias: float32 [1280], P('blk'), may hold values from -3 to 3
- cotangent: bfloat16 [64, 1280, 256], P('dp', 'blk'), may hold values from -6 to 6
Outputs:
- response: bfloat16 [64, 1280, 256], P('dp', 'blk')
- frame_grad: bfloat16 [64, 1280, 256], P('dp', 'blk')
- weight_grad: float32 [1280, 11520], P(('blk', 'dp'))
All inputs are finite; a program needn't handle non-finite values.
Results may differ from a plain program's by a relative error of at most 0.001.
Values may be sent and summed in bfloat16 or wider, within the bound.
A program may use at most 128 MiB of HBM per device.

v0:
```python
import jax
import jax.numpy as jnp
from jax import lax
from jax.sharding import PartitionSpec as P

WD = 16


def shift_cells(maps, step_row, step_col):
    cells = maps.shape[-1]
    margin = WD + 1
    widths = [(0, 0)] * (maps.ndim - 1) + [(margin, margin)]
    flat = jnp.pad(maps, widths)
    begin = margin + step_row * WD + step_col
    moved = lax.slice_in_dim(flat, begin, begin + cells, axis=maps.ndim - 1)
    column = jnp.arange(cells, dtype=jnp.int32) % WD + step_col
    keeper = ((column >= 0) & (column < WD)).astype(maps.dtype)
    return moved * keeper


def body(frames, weight, bias, cotangent):
    nframe = frames.shape[0]
    local_ch = frames.shape[1]
    cells = frames.shape[2]
    whole = lax.all_gather(frames, "blk", axis=1, tiled=True)
    all_ch = whole.shape[1]
    total = jnp.zeros((nframe, local_ch, cells), jnp.float32)
    grads = []
    for tap in range(9):
        ky, kx = divmod(tap, 3)
        piece = shift_cells(whole, ky - 1, kx - 1)
        w_tap = weight[:, tap * all_ch : (tap + 1) * all_ch]
        total = total + jnp.einsum("oi,fic->foc", w_tap, piece, preferred_element_type=jnp.float32)
        grads.append(
            lax.dot_general(
                cotangent, piece, (((0, 2), (0, 2)), ((), ())), preferred_element_type=jnp.float32
            )
        )
    response = (total + bias[None, :, None]).astype(jnp.bfloat16)
    local_grad = jnp.concatenate(grads, axis=1)
    weight_grad = lax.psum_scatter(local_grad, "dp", scatter_dimension=0, tiled=True)
    cot_moved = [shift_cells(cotangent, 1 - tap // 3, 1 - tap % 3) for tap in range(9)]
    accum = jnp.zeros((lax.axis_size("blk") * local_ch, nframe, cells), jnp.float32)
    for tap in range(9):
        w_cols = lax.dynamic_slice_in_dim(weight, tap * all_ch, lax.axis_size("blk") * local_ch, 1)
        accum = accum + jnp.einsum(
            "oi,foc->ifc", w_cols, cot_moved[tap], preferred_element_type=jnp.float32
        )
    shares = lax.psum_scatter(accum, "blk", scatter_dimension=0, tiled=True)
    frame_grad = jnp.transpose(shares, (1, 0, 2)).astype(jnp.bfloat16)
    return (response, frame_grad, weight_grad)


def solution(mesh):
    return jax.shard_map(
        body,
        mesh=mesh,
        in_specs=(P("dp", "blk", None), P("blk", None), P("blk"), P("dp", "blk", None)),
        out_specs=(P("dp", "blk", None), P("dp", "blk", None), P(("blk", "dp"), None)),
        check_vma=False,
    )
```

profile of v0, /device:TPU:1, one launch (start us, length us, event | category | flops | bytes accessed | tf_op | source)
XLA Modules:
  0.0 334.2 jit_solution(7435251085042753717)
XLA Ops:
  7.2 0.0 all-gather.2.cloned.1.call-start
  7.2 0.7 all-gather.2.cloned.1.call-update
  7.9 0.0 all-reduce.7.cloned.1.call-start
  8.0 0.0 copy-start
  8.0 0.0 copy-start.2
  8.0 2.2 fusion.100
  10.2 0.0 copy-done
  10.2 0.0 copy-done.2
  10.2 3.3 fusion.109
  13.5 3.3 fusion.103
  16.8 3.4 %fusion.112 = f32[4,256,1280]{2,1,0:T(8,128)} fusion(bf16[80,11520]{1,0:T(8,128)(2,1)S(1)} %copy-done.2, bf16[4,80,256]{2,1,0:T(8,128)(2,1)S(1)} %copy-done, bf16[256]{0:T(256)(128)(2,1)S(1)} %and_convert_fusion.2), kind=kOutput, calls=%fused_computation.101 | convolution fusion | flops 210042880 | bytes 5612032 | tf_op jit(solution)/shard_map/oi,foc->ifc/dot_general | solution.py:46
  20.2 3.3 fusion.118
  23.4 3.3 fusion.115
  26.8 3.3 fusion.97
  30.0 3.3 fusion.106
  33.3 15.3 %add_bitcast_fusion = f32[1280,4,256]{0,2,1:T(8,128)} fusion(f32[4,256,1280]{2,1,0:T(8,128)} %fusion.97, f32[4,256,1280]{2,1,0:T(8,128)S(1)} %fusion.100, f32[4,256,1280]{2,1,0:T(8,128)} %fusion.103, f32[4,256,1280]{2,1,0:T(8,128)} %fusion.106, f32[4,256,1280]{2,1,0:T(8,128)} %fusion.109, f32[4,256,1280]{2,1,0:T(8,128)} %fusion.112, ...), kind=kOutput, calls=%fused_computation.8 | convolution fusion | flops 220528640 | bytes 47555072 | tf_op jit(solution)/shard_map/oi,foc->ifc/dot_general | solution.py:46
  48.6 7.2 %copy.8 = f32[1280,4,256]{2,1,0:T(4,128)} copy(f32[1280,4,256]{0,2,1:T(8,128)} %add_bitcast_fusion) | data formatting | bytes 10485760 | tf_op jit(solution)/shard_map/add | solution.py:46
  55.8 0.0 copy-done.6
  55.8 0.6 dynamic-slice
  57.1 0.0 copy-start.5
  57.1 120.9 %all-reduce.8 = bf16[1280,4,256]{2,1,0:T(4,128)(2,1)S(1)} all-reduce(f32[1280,4,256]{2,1,0:T(4,128)} %copy.8), channel_id=2, replica_groups=mesh['dp'=16,'blk'=16] {'blk'}, use_global_device_ids=true, to_apply=%region_0.1.clone | all-reduce | flops 1310720 | bytes 7864320
  177.9 0.1 fusion.139
  178.0 0.7 copy.9
  178.7 0.6 dynamic-slice.2
  179.9 0.0 all-gather.2.cloned.1.call-done
  180.0 3.9 %fusion.16 = f32[80,11520]{1,0:T(8,128)} fusion(bf16[4,80,256]{2,1,0:T(8,128)(2,1)S(1)} %copy-done, bf16[4,1280,256]{2,1,0:T(8,128)(2,1)} %all-gather.2.cloned.1.call-done, bf16[256]{0:T(256)(128)(2,1)S(1)} %and_convert_fusion.2), kind=kOutput, calls=%fused_computation.34 | convolution fusion | flops 214958080 | bytes 3195392 | tf_op jit(solution)/shard_map/dot_general | solution.py:35
  183.9 2.0 fusion.15
  186.0 2.0 fusion.14
  188.0 2.0 fusion.13
  190.0 1.7 fusion.12
  191.7 2.0 fusion.11
  193.8 2.0 fusion.10
  195.8 2.1 fusion.9
  197.8 2.0 fusion.8
  199.8 0.0 all-reduce.7.cloned.1.call-update
  199.9 0.0 copy-start.3
  199.9 2.2 fusion.39
  202.1 1.1 fusion.21
  203.2 1.1 fusion.24
  204.2 1.3 fusion.27
  205.5 1.1 fusion.30
  206.6 1.1 fusion.77
  207.7 1.1 fusion.80
  208.8 0.0 copy-start.4
  208.8 1.1 fusion.83
  209.9 1.4 fusion.92
  211.3 114.1 %all-reduce.7.cloned.1.call-done = f32[80,11520]{1,0:T(8,128)} async-done(((f32[80,11520]{1,0:T(8,128)}), f32[80,11520]{1,0:T(8,128)}) %all-reduce.7.cloned.1.call-update) | async-done | bytes 3686416
  325.4 1.9 constant_dynamic-slice_fusion
  (9 shorter events, 0.0 us)
Async XLA Ops:
  7.2 172.8 %all-gather.2.cloned.1.call-start = ((), (), s32[]{:S(2)}) async-start(), calls=%async_computation | async-start | bytes 2785280 | tf_op jit(solution)/shard_map/all_gather | solution.py:25
  7.9 317.5 %all-reduce.7.cloned.1.call-start = ((), (), s32[]{:S(2)}) async-start(), calls=%async_computation.1 | async-start | bytes 7372800
  8.0 2.2 copy-start
  8.0 2.2 copy-start.2
  48.6 7.2 %copy-start.6 = (u32[256]{0:T(256)S(1)}, u32[256]{0:T(256)}, u32[]{:S(2)}) copy-start(u32[256]{0:T(256)} %constant.84) | copy-start | bytes 3076
  57.1 121.6 %copy-start.5 = (u32[256]{0:T(256)S(1)}, u32[256]{0:T(256)}, u32[]{:S(2)}) copy-start(u32[256]{0:T(256)} %constant.88) | copy-start | bytes 3076
  180.0 4.0 %copy-start.1 = (bf16[4,1280,256]{2,1,0:T(8,128)(2,1)S(1)}, bf16[4,1280,256]{2,1,0:T(8,128)(2,1)}, u32[]{:S(2)}) copy-start(bf16[4,1280,256]{2,1,0:T(8,128)(2,1)} %all-gather.2.cloned.1.call-done) | copy-start | bytes 7864324
  199.9 2.2 copy-start.3
  208.8 1.1 copy-start.4
Sparse Core Ops, SparseCore 0:
  10.4 54.7 all-gather.1
  200.0 125.4 all-reduce.6
where the time goes:
time: 335 us; the launch traced here: 334 us
  blocking collectives  121 us (36%)
  waiting for transfers between devices  115 us (34%)
  matrix products  71.8 us (21%)
  between operations  15.5 us (5%)
  local copies, waits for them, and re-layouts  11.1 us (3%)
    unnamed x1, blocking collectives  121 us
    unnamed x3, waiting for transfers between devices  115 us
    dot_general x9, matrix products, body(): jnp.einsum('oi,foc->ifc', w_cols, cot_moved[tap], preferred_element_type=...  40.6 us
    dot_general x9, matrix products, body(): lax.dot_general(cotangent, piece, (((0, 2), (0, 2)), ((), ())), preferred...  19.9 us
    dot_general x9, matrix products, body(): jnp.einsum('oi,fic->foc', w_tap, piece, preferred_element_type=jnp.float32)  11.4 us
    add x1, local copies, waits for them, and re-layouts, body(): accum + jnp.einsum('oi,foc->ifc', w_cols, cot_moved[tap], preferred_eleme...  7.21 us
  transfers between devices with their start and end apart: 2, of which 1 were waited for; matrix products, arithmetic and copies ran while one was open for 18% of the time, Pallas kernels for 0%

commit v1 on v0

v1 whole, which is shorter than its diff:
```python
import functools

import jax
import jax.numpy as jnp
import ml_dtypes
import numpy as np
from jax import lax
from jax.experimental import pallas as pl
from jax.experimental.pallas import tpu as pltpu
from jax.sharding import PartitionSpec as P

MESH = pl.DeviceIdType.MESH
CH = 80
NB = 16
C = CH * NB
TAPS = 9
CELLS = 256
NF = 4
PAD = 768
HALF = 384
ROWS = 48
NQ = 5

RELAYS = [(1, 0), (3, 0), (0, 1), (2, 0), (1, 1), (3, 1), (2, 1)]
LEAVES = [(0, 3), (1, 3), (3, 3), (2, 3), (0, 2), (1, 2), (3, 2), (2, 2)]
TREES = [(True, 1), (True, -1), (False, 1), (False, -1)]


def offsets(tap):
    return tap // 3 - 1, tap % 3 - 1


def moved(v, dy, dx):
    if dy == 0 and dx == 0:
        return v
    cell = lax.broadcasted_iota(jnp.int32, (1, CELLS), 1)
    h = lax.shift_right_logical(cell, 4) + dy
    w = lax.bitwise_and(cell, 15) + dx
    keep = (h >= 0) & (h < 16) & (w >= 0) & (w < 16)
    rolled = pltpu.roll(v, (-(dy * 16 + dx)) % CELLS, axis=1)
    return jnp.where(keep, rolled, jnp.zeros_like(rolled))


def kernel(nz, frames_hbm, weight_hbm, bias_ref, cot_hbm, perm_ref,
           resp_ref, fgrad_ref, wgrad_ref,
           g, ws, pb, r, rt, cst, csp, pw, mb, s, rp,
           lsem, wlsem, ag_s, ag_r, w_s, w_r, d_s, d_r, m_s, m_r, rs_s, rs_r):
    dp = lax.axis_index("dp")
    blk = lax.axis_index("blk")
    z, core = dp // 2, lax.rem(dp, 2)
    y, x = blk // 4, lax.rem(blk, 4)
    sib = (z * 2 + 1 - core, blk)

    def plane(b):
        return (dp, b)

    def zdev(step):
        return (lax.rem(z + step + nz, nz) * 2 + core, blk)

    loads = []
    for a, src in enumerate((frames_hbm, cot_hbm)):
        for f in range(NF):
            cp = pltpu.make_async_copy(
                src.at[f], g.at[a, f, pl.ds(pl.multiple_of(blk * CH, 16), CH), :], lsem.at[a, f])
            cp.start()
            loads.append(cp)
    wloads = []
    for t in range(TAPS):
        cp = pltpu.make_async_copy(
            weight_hbm.at[:, pl.ds(t * C, C)], ws.at[pl.ds(t * CH, CH), :], wlsem.at[t])
        cp.start()
        wloads.append(cp)

    barrier = pltpu.get_barrier_semaphore()
    for k in range(1, NB):
        pl.semaphore_signal(barrier, inc=1, device_id=plane(lax.rem(blk + k, NB)), device_id_type=MESH)
    for dev in (sib, zdev(1), zdev(-1)):
        pl.semaphore_signal(barrier, inc=1, device_id=dev, device_id_type=MESH)
    for cp in loads:
        cp.wait()
    pl.semaphore_wait(barrier, NB + 2)

    pending = []

    def remote(src, dst, ssem, rsem, dev):
        cp = pltpu.make_async_remote_copy(
            src_ref=src, dst_ref=dst, send_sem=ssem, recv_sem=rsem,
            device_id=dev, device_id_type=MESH)
        cp.start()
        pending.append(cp)

    def at(tree, step_a, step_b):
        first_x, _ = TREES[tree]
        sx, sy = (step_a, step_b) if first_x else (step_b, step_a)
        return lax.rem(y + sy + 4, 4) * 4 + lax.rem(x + sx + 4, 4)

    def block(a, f, ra, rb):
        sgn = TREES[f][1]
        src = at(f, -sgn * (ra if ra < 3 else -1), -sgn * (rb if rb < 3 else -1))
        return g.at[a, f, pl.ds(pl.multiple_of(src * CH, 16), CH), :]

    counts = {}

    def push(a, f, ra, rb, along_a, forward):
        n = counts.get((a, f), 0)
        counts[(a, f)] = n + 1
        sgn = TREES[f][1]
        step = sgn if forward else -sgn
        dev = at(f, step, 0) if along_a else at(f, 0, step)
        if along_a:
            there = (ra + 1 if forward else 3, rb)
        else:
            there = (ra, rb + 1 if forward else 3)
        ref = block(a, f, ra, rb)
        remote(ref, ref, ag_s.at[a, f, n], ag_r.at[a, f, there[0] * 4 + there[1]], plane(dev))

    def arrived(a, f, ra, rb):
        ref = block(a, f, ra, rb)
        pltpu.make_async_remote_copy(
            src_ref=ref, dst_ref=ref, send_sem=ag_s.at[a, f, 0],
            recv_sem=ag_r.at[a, f, ra * 4 + rb], device_id=plane(at(f, 1, 0)),
            device_id_type=MESH).wait_recv()

    def own_sends(a):
        for f in range(NF):
            push(a, f, 0, 0, True, True)
            push(a, f, 0, 0, False, True)
            push(a, f, 0, 0, True, False)
            push(a, f, 0, 0, False, False)

    def relay(a, event):
        ra, rb = event
        for f in range(NF):
            arrived(a, f, ra, rb)
            if rb == 0:
                if ra == 1:
                    push(a, f, ra, rb, True, True)
                push(a, f, ra, rb, False, True)
                push(a, f, ra, rb, False, False)
            elif rb == 1:
                push(a, f, ra, rb, False, True)

    def leaves(a, event):
        for f in range(NF):
            arrived(a, f, *event)

    own_sends(0)

    for cp in wloads:
        cp.wait()

    def pack(half):
        for b in range(NB):
            parts = []
            for t in range(TAPS):
                lo, hi = max(t * CH, half * HALF), min((t + 1) * CH, (half + 1) * HALF)
                if lo < hi:
                    parts.append(ws[t * CH:(t + 1) * CH, b * CH + lo - t * CH:b * CH + hi - t * CH])
            if half == 1:
                parts.append(jnp.zeros((CH, PAD - TAPS * CH), jnp.bfloat16))
            pb[b] = jnp.concatenate(parts, axis=1)

    @pl.when(core == 0)
    def _():
        pack(0)

    @pl.when(core == 1)
    def _():
        pack(1)

    mine = pl.ds(pl.multiple_of(blk * CH, 16), CH)
    own_w = pltpu.make_async_copy(pb.at[blk], r.at[core, mine, :], w_s.at[0])
    own_w.start()
    for k in range(1, NB):
        b = lax.rem(blk + k, NB)
        remote(pb.at[b], r.at[core, mine, :], w_s.at[k], w_r.at[k], plane(b))

    relay(0, RELAYS[0])
    relay(0, RELAYS[1])
    relay(0, RELAYS[2])
    relay(0, RELAYS[3])

    def shifted(f):
        cot = g[1, f, mine, :].astype(jnp.float32)
        for t in range(TAPS):
            dy, dx = offsets(t)
            cst[t * CH:(t + 1) * CH, :] = moved(cot, -dy, -dx).astype(jnp.bfloat16)
        csp[:, f * CELLS:(f + 1) * CELLS] = jnp.dot(
            perm_ref[...], cst[...], preferred_element_type=jnp.float32).astype(jnp.bfloat16)

    shifted(0)
    relay(0, RELAYS[4])
    shifted(1)
    relay(0, RELAYS[5])
    shifted(2)
    relay(0, RELAYS[6])
    own_sends(1)
    shifted(3)
    for ev in LEAVES:
        leaves(0, ev)
    relay(1, RELAYS[0])
    relay(1, RELAYS[1])

    for q in range(NQ):
        acc = None
        for f in range(NF):
            part = lax.dot_general(
                csp[:, f * CELLS:(f + 1) * CELLS], g[0, f, q * 256:(q + 1) * 256, :],
                (((1,), (1,)), ((), ())), preferred_element_type=jnp.float32)
            acc = part if acc is None else acc + part
        for c in range(2):
            pw[c, q] = acc[c * nz * ROWS:(c + 1) * nz * ROWS].reshape(nz, ROWS, 256)
        remote(pw.at[1 - core, q], mb.at[q], m_s.at[q], m_r.at[q], sib)
        relay(1, RELAYS[2 + q])

    def hops(q, forward):
        return 4 if (q % 2 == 0) == forward else 3

    def rs_send(q, forward, k):
        n = hops(q, forward)
        i = 0 if forward else 1
        dist = n - k
        to = lax.rem(z + dist, nz) if forward else lax.rem(z - dist + nz, nz)
        if k > 0:
            rs_wait(q, forward, k - 1)
            s[q, to] = s[q, to] + rp[i, q, k - 1]
        remote(s.at[q, to], rp.at[i, q, k], rs_s.at[i, q, k], rs_r.at[i, q, k],
               zdev(1 if forward else -1))

    def rs_wait(q, forward, k):
        i = 0 if forward else 1
        ref = rp.at[i, q, k]
        pltpu.make_async_remote_copy(
            src_ref=ref, dst_ref=ref, send_sem=rs_s.at[i, q, k], recv_sem=rs_r.at[i, q, k],
            device_id=zdev(1), device_id_type=MESH).wait_recv()

    for q in range(NQ):
        pltpu.make_async_remote_copy(
            src_ref=mb.at[q], dst_ref=mb.at[q], send_sem=m_s.at[q], recv_sem=m_r.at[q],
            device_id=sib, device_id_type=MESH).wait_recv()
        for k in range(nz):
            s[q, k] = pw[core, q, k] + mb[q, k]
        rs_send(q, True, 0)
        rs_send(q, False, 0)

    def forward_conv(a, f, lhs, sign):
        prod = jnp.dot(lhs[0:TAPS * CH, :], g[a, f], preferred_element_type=jnp.float32)
        total = None
        for t in range(TAPS):
            dy, dx = offsets(t)
            term = moved(prod[t * CH:(t + 1) * CH], sign * dy, sign * dx)
            total = term if total is None else total + term
        return total

    def respond(f):
        resp_ref[f] = (forward_conv(0, f, ws, 1) + bias_ref[...]).astype(jnp.bfloat16)

    def rs_round(k):
        for q in range(NQ):
            for forward in (True, False):
                if k < hops(q, forward):
                    rs_send(q, forward, k)

    for f in range(NF):
        respond(f)
        if f == 1:
            rs_round(1)
    for ev in LEAVES:
        leaves(1, ev)
    rs_round(2)

    own_w.wait()
    for k in range(1, NB):
        pltpu.make_async_remote_copy(
            src_ref=pb.at[0], dst_ref=r.at[core, pl.ds(0, CH), :], send_sem=w_s.at[k],
            recv_sem=w_r.at[k], device_id=sib, device_id_type=MESH).wait_recv()
    remote(r.at[core], r.at[core], d_s.at[0], d_r.at[0], sib)

    def turn(half):
        rt[pl.ds(pl.multiple_of(half * HALF, 128), HALF), :] = r[half].T

    turn(core)
    pltpu.make_async_remote_copy(
        src_ref=r.at[1 - core], dst_ref=r.at[1 - core], send_sem=d_s.at[0], recv_sem=d_r.at[0],
        device_id=sib, device_id_type=MESH).wait_recv()
    turn(1 - core)

    for f in range(NF):
        fgrad_ref[f] = forward_conv(1, f, rt, -1).astype(jnp.bfloat16)
        if f == 0:
            rs_round(3)

    for q in range(NQ):
        rs_wait(q, True, hops(q, True) - 1)
        rs_wait(q, False, hops(q, False) - 1)
        final = s[q, z] + rp[0, q, hops(q, True) - 1] + rp[1, q, hops(q, False) - 1]
        for t in range(TAPS):
            wgrad_ref[:, t * C + q * 256:t * C + (q + 1) * 256] = final[t * 5:(t + 1) * 5]

    for cp in pending:
        cp.wait_send()


def solution(mesh):
    nz = mesh.shape["dp"] // 2
    table = np.zeros((PAD, TAPS * CH), np.float32)
    for c in range(2):
        for k in range(nz):
            for t in range(TAPS):
                for j in range(5):
                    table[c * nz * ROWS + k * ROWS + t * 5 + j, t * CH + k * 10 + c * 5 + j] = 1
    table = table.astype(ml_dtypes.bfloat16)

    bf16, f32 = jnp.bfloat16, jnp.float32
    vmem = pl.BlockSpec(memory_space=pltpu.VMEM)
    hbm = pl.BlockSpec(memory_space=pl.ANY)
    dma = pltpu.SemaphoreType.DMA

    def body(frames, weight, bias, cotangent):
        return pl.pallas_call(
            functools.partial(kernel, nz),
            out_shape=(
                jax.ShapeDtypeStruct((NF, CH, CELLS), bf16),
                jax.ShapeDtypeStruct((NF, CH, CELLS), bf16),
                jax.ShapeDtypeStruct((5, TAPS * C), f32),
            ),
            in_specs=[hbm, hbm, vmem, hbm, vmem],
            out_specs=(vmem, vmem, vmem),
            scratch_shapes=[
                pltpu.VMEM((2, NF, C, CELLS), bf16),
                pltpu.VMEM((TAPS * CH, C), bf16),
                pltpu.VMEM((NB, CH, HALF), bf16),
                pltpu.VMEM((2, C, HALF), bf16),
                pltpu.VMEM((PAD, C), bf16),
                pltpu.VMEM((TAPS * CH, CELLS), bf16),
                pltpu.VMEM((PAD, NF * CELLS), bf16),
                pltpu.VMEM((2, NQ, nz, ROWS, 256), f32),
                pltpu.VMEM((NQ, nz, ROWS, 256), f32),
                pltpu.VMEM((NQ, nz, ROWS, 256), f32),
                pltpu.VMEM((2, NQ, 4, ROWS, 256), f32),
                dma((2, NF)), dma((TAPS,)),
                dma((2, NF, 15)), dma((2, NF, 16)),
                dma((NB,)), dma((NB,)),
                dma((1,)), dma((1,)),
                dma((NQ,)), dma((NQ,)),
                dma((2, NQ, 4)), dma((2, NQ, 4)),
            ],
            compiler_params=pltpu.CompilerParams(
                collective_id=0, has_side_effects=True, vmem_limit_bytes=60 * 1024 * 1024),
        )(frames, weight, bias[:, None], cotangent, jnp.asarray(table))

    return jax.shard_map(
        body,
        mesh=mesh,
        in_specs=(P("dp", "blk", None), P("blk", None), P("blk"), P("dp", "blk", None)),
        out_specs=(P("dp", "blk", None), P("dp", "blk", None), P(("blk", "dp"), None)),
        check_vma=False,
    )
```

time: 335 us -> 82.3 us (0.25)
  blocking collectives: 121 us -> 0 us
  waiting for transfers between devices: 115 us -> 0 us
  Pallas kernels: 0 us -> 75.1 us
  matrix products: 71.8 us -> 0 us
  between operations: 15.5 us -> 0.64 us
  local copies, waits for them, and re-layouts: 11.1 us -> 6.3 us
    unnamed x1 -> x0, blocking collectives: 121 us -> none
    unnamed x3 -> x0, waiting for transfers between devices: 115 us -> none
    pallas_call x0 -> x1, Pallas kernels: none -> 75.1 us  [body(): pl.pallas_call(functools.partial(kernel, nz), out_shape=(jax.ShapeDtypeSt...]
    dot_general x27 -> x0, matrix products: 71.8 us -> none  [the longest x9 40.6 us: body(): jnp.einsum('oi,foc->ifc', w_cols, cot_moved[tap], preferred_element_type=...]
    add x1 -> x0, local copies, waits for them, and re-layouts: 7.21 us -> none  [body(): accum + jnp.einsum('oi,foc->ifc', w_cols, cot_moved[tap], preferred_eleme...]
  transfers between devices with their start and end apart: 2 -> 0, of which waited for: 1 -> 0; matrix products, arithmetic and copies ran while one was open for 18% -> 0% of each run, Pallas kernels for 0% -> 0%
where the time goes in v1:
time: 82.3 us; the launch traced here: 82 us
  Pallas kernels  75.1 us (91%)
  local copies, waits for them, and re-layouts  6.3 us (8%)
    pallas_call x1, Pallas kernels, body(): pl.pallas_call(functools.partial(kernel, nz), out_shape=(jax.ShapeDtypeSt...  75.1 us
    unnamed x3, local copies, waits for them, and re-layouts  4.93 us

profile of v1, /device:TPU:1, one launch (start us, length us, event | category | flops | bytes accessed | tf_op | source)
XLA Modules:
  0.0 82.0 jit_solution(17698352439477718025)
XLA Ops:
  0.6 1.4 %copy.8.bias_ref = f32[80,1]{1,0:T(8,128)} copy(f32[80,1]{0,1:T(1,128)} %bitcast.1) | data formatting | bytes 640 | tf_op jit(solution)/shard_map/broadcast_in_dim | solution.py:350
  2.0 75.1 %shard_map.76 = (bf16[4,80,256]{2,1,0:T(8,128)(2,1)}, bf16[4,80,256]{2,1,0:T(8,128)(2,1)}, f32[5,11520]{1,0:T(8,128)}) custom-call(bf16[4,80,256]{2,1,0:T(8,128)(2,1)} %frames_hbm.1, bf16[80,11520]{1,0:T(8,128)(2,1)} %weight_hbm.1, f32[80,1]{1,0:T(8,128)} %copy.8.bias_ref, bf16[4,80,256]{2,1,0:T(8,128)(2,1)} %cot_hbm.1, bf16[768,720]{1,0:T(8,128)(2,1)} %constant.2.clone.perm_ref), custom_call_target="tpu_custom_call" | custom-call | tf_op jit(solution)/shard_map/pallas_call | solution.py:320
  77.1 1.6 %copy.12 = bf16[4,80,256]{2,1,0:T(8,128)(2,1)} copy(bf16[4,80,256]{2,1,0:T(8,128)(2,1)} %get-tuple-element.6) | data formatting | bytes 327680
  78.7 1.6 %copy.13 = bf16[4,80,256]{2,1,0:T(8,128)(2,1)} copy(bf16[4,80,256]{2,1,0:T(8,128)(2,1)} %get-tuple-element.7) | data formatting | bytes 327680
  80.3 1.7 %copy.14 = f32[5,11520]{1,0:T(8,128)} copy(f32[5,11520]{1,0:T(8,128)} %get-tuple-element.8) | data formatting | bytes 460800

commit v2 on v0

v2 whole, which is shorter than its diff:
```python
import functools

import jax
import jax.numpy as jnp
import ml_dtypes
import numpy as np
from jax import lax
from jax.experimental import pallas as pl
from jax.experimental.pallas import tpu as pltpu
from jax.sharding import PartitionSpec as P

MESH = pl.DeviceIdType.MESH
CH = 80
NB = 16
C = CH * NB
TAPS = 9
CELLS = 256
NF = 4
PAD = 768
ROWS = 48
BAND = 320

TREES = [(True, 1), (True, -1), (False, 1), (False, -1)]
BANDS = [0, 1, -1, 2]
CHUNKS = [(0, 256, 4), (256, 384, 3), (640, 256, 3), (896, 384, 4)]


def offsets(tap):
    return tap // 3 - 1, tap % 3 - 1


def moved(v, dy, dx):
    if dy == 0 and dx == 0:
        return v
    cell = lax.broadcasted_iota(jnp.int32, (1, CELLS), 1)
    h = lax.shift_right_logical(cell, 4) + dy
    w = lax.bitwise_and(cell, 15) + dx
    keep = (h >= 0) & (h < 16) & (w >= 0) & (w < 16)
    rolled = pltpu.roll(v, (-(dy * 16 + dx)) % CELLS, axis=1)
    return jnp.where(keep, rolled, jnp.zeros_like(rolled))


def kernel(nz, frames_hbm, weight_hbm, bias_ref, cot_hbm, perm_hbm,
           resp_hbm, fgrad_hbm, wgrad_hbm,
           g, ws, pb, r, rt, perm, cst, csp, resp, fgrad, wgrad,
           pw0, pw1, pw2, pw3, mb0, mb1, mb2, mb3, rp0, rp1, rp2, rp3,
           lsem, wlsem, osem, ag_s, ag_r, w_s, w_r, z_s, z_r, d_s, d_r,
           m_s, m_r, rs_s, rs_r):
    pw, mb, rp = (pw0, pw1, pw2, pw3), (mb0, mb1, mb2, mb3), (rp0, rp1, rp2, rp3)
    dp = lax.axis_index("dp")
    blk = lax.axis_index("blk")
    z, core = dp // 2, lax.rem(dp, 2)
    y, x = blk // 4, lax.rem(blk, 4)
    sib = (z * 2 + 1 - core, blk)

    def plane(b):
        return (dp, b)

    def zdev(step):
        return (lax.rem(z + step + nz, nz) * 2 + core, blk)

    def mine(a, f):
        return g.at[a, f, pl.ds(pl.multiple_of(blk * CH, 16), CH), :]

    loads = {}

    def load(name, src, dst, sem):
        loads[name] = pltpu.make_async_copy(src, dst, sem)
        loads[name].start()

    for a, src in enumerate((frames_hbm, cot_hbm)):
        for f in range(NF):
            load((a, f), src.at[f], mine(a, f), lsem.at[a, f])
    for t in range(TAPS):
        load(t, weight_hbm.at[:, pl.ds(t * C, C)], ws.at[pl.ds(t * CH, CH), :], wlsem.at[t])
    load("perm", perm_hbm, perm, wlsem.at[TAPS])

    barrier = pltpu.get_barrier_semaphore()
    for k in range(1, NB):
        pl.semaphore_signal(barrier, inc=1, device_id=plane(lax.rem(blk + k, NB)), device_id_type=MESH)
    for dev in (sib, zdev(1), zdev(-1)):
        pl.semaphore_signal(barrier, inc=1, device_id=dev, device_id_type=MESH)
    for a in range(2):
        for f in range(NF):
            loads[a, f].wait()
    pl.semaphore_wait(barrier, NB + 2)

    pending = []

    def remote(src, dst, ssem, rsem, dev):
        cp = pltpu.make_async_remote_copy(
            src_ref=src, dst_ref=dst, send_sem=ssem, recv_sem=rsem,
            device_id=dev, device_id_type=MESH)
        cp.start()
        pending.append(cp)

    def wait_for(ref, ssem, rsem):
        pltpu.make_async_remote_copy(
            src_ref=ref, dst_ref=ref, send_sem=ssem, recv_sem=rsem,
            device_id=sib, device_id_type=MESH).wait_recv()

    def at(tree, step_a, step_b):
        first_x, _ = TREES[tree]
        sx, sy = (step_a, step_b) if first_x else (step_b, step_a)
        return lax.rem(y + sy + 4, 4) * 4 + lax.rem(x + sx + 4, 4)

    def block(a, f, ra, rb):
        sgn = TREES[f][1]
        src = at(f, -sgn * (ra if ra < 3 else -1), -sgn * (rb if rb < 3 else -1))
        return g.at[a, f, pl.ds(pl.multiple_of(src * CH, 16), CH), :]

    counts = {}

    def push(a, f, ra, rb, along_a, forward):
        n = counts.get((a, f), 0)
        counts[(a, f)] = n + 1
        sgn = TREES[f][1]
        step = sgn if forward else -sgn
        dev = at(f, step, 0) if along_a else at(f, 0, step)
        if along_a:
            there = (ra + 1 if forward else 3, rb)
        else:
            there = (ra, rb + 1 if forward else 3)
        ref = block(a, f, ra, rb)
        remote(ref, ref, ag_s.at[a, f, n], ag_r.at[a, f, there[0] * 4 + there[1]], plane(dev))

    seen = set()

    def need(a, f, ra, rb):
        if (a, f, ra, rb) in seen or (ra, rb) == (0, 0):
            return
        seen.add((a, f, ra, rb))
        wait_for(block(a, f, ra, rb), ag_s.at[a, f, 0], ag_r.at[a, f, ra * 4 + rb])
        if rb == 0:
            if ra == 1:
                push(a, f, ra, rb, True, True)
            push(a, f, ra, rb, False, True)
            push(a, f, ra, rb, False, False)
        elif rb == 1:
            push(a, f, ra, rb, False, True)

    def events(a, *pairs):
        for ra, rb in pairs:
            for f in range(NF):
                need(a, f, ra, rb)

    def band(a, step):
        for f in range(NF):
            first_x, sgn = TREES[f]
            code = {0: 0, 2: 2, -sgn: 1, sgn: 3}[step]
            for other in (0, 1, 3, 2):
                need(a, f, *((other, code) if first_x else (code, other)))

    def own_sends(a):
        for f in range(NF):
            push(a, f, 0, 0, True, True)
            push(a, f, 0, 0, False, True)
            push(a, f, 0, 0, True, False)
            push(a, f, 0, 0, False, False)

    def band_rows(k):
        return pl.multiple_of(lax.rem(y + BANDS[k] + 4, 4) * BAND, 64)

    def shifted(f):
        cot = mine(1, f)[...].astype(jnp.float32)
        for t in range(TAPS):
            dy, dx = offsets(t)
            cst[t * CH:(t + 1) * CH, :] = moved(cot, -dy, -dx).astype(jnp.bfloat16)
        csp[:, f * CELLS:(f + 1) * CELLS] = jnp.dot(
            perm[...], cst[...], preferred_element_type=jnp.float32).astype(jnp.bfloat16)

    def piece_of(zz, cc):
        d = zz * 2 + cc
        return d // 3, lax.rem(d, 3)

    my_row, my_group = piece_of(z, core)
    row_start = pl.multiple_of(jnp.minimum(my_row, 4) * 16, 16)

    def pack(group):
        for b in range(NB):
            parts = []
            for t in range(TAPS):
                lo, hi = max(t * CH, group * 256), min((t + 1) * CH, (group + 1) * 256)
                if lo < hi:
                    parts.append(ws[pl.ds(pl.multiple_of(t * CH + row_start, 16), 16),
                                    b * CH + lo - t * CH:b * CH + hi - t * CH])
            if group == 2:
                parts.append(jnp.zeros((16, PAD - TAPS * CH), jnp.bfloat16))
            pb[b] = jnp.concatenate(parts, axis=1)

    def send_slices():
        for group in range(3):
            @pl.when(my_group == group)
            def _(group=group):
                pack(group)
        own = pltpu.make_async_copy(pb.at[blk], r.at[blk, my_row, my_group], w_s.at[0])
        own.start()
        for k in range(1, NB):
            b = lax.rem(blk + k, NB)
            remote(pb.at[b], r.at[blk, my_row, my_group], w_s.at[k], w_r.at[k], plane(b))
        return own

    def z_piece(i, k, cc):
        zz = lax.rem(z + (-k if i == 0 else k) + nz, nz)
        row, group = piece_of(zz, cc)
        part = pl.ds(0, NB) if k < 4 else pl.ds(i * 8, 8)
        return r.at[part, row, group]

    def z_push(i, k):
        zz = lax.rem(z + (-k if i == 0 else k) + nz, nz)
        row, group = piece_of(zz, core)
        part = pl.ds(0, NB) if k < 3 else pl.ds(i * 8, 8)
        ref = r.at[part, row, group]
        remote(ref, ref, z_s.at[i, k], z_r.at[i, k + 1], zdev(1 if i == 0 else -1))

    def z_start(own):
        own.wait()
        for k in range(1, NB):
            wait_for(pb.at[0], w_s.at[k], w_r.at[k])
        z_push(0, 0)
        z_push(1, 0)
        ref = r.at[:, my_row, my_group]
        remote(ref, ref, d_s.at[0, 0], d_r.at[0, 0], sib)

    def z_relay(k):
        for i in range(2):
            wait_for(z_piece(i, k, core), z_s.at[i, 0], z_r.at[i, k])
            if k < 4:
                z_push(i, k)
            ref = z_piece(i, k, core)
            remote(ref, ref, d_s.at[i, k], d_r.at[i, k], sib)

    def z_finish():
        for i in range(2):
            for k in range(5):
                if (i, k) != (1, 0):
                    wait_for(z_piece(i, k, 1 - core), d_s.at[0, 0], d_r.at[i, k])

    def turn(group):
        m = jnp.concatenate(
            [r[pl.ds(lax.rem(y + step + 4, 4) * 4, 4), 0:5, group].reshape(BAND, 256) for step in BANDS], axis=0)
        rt[group * 256:(group + 1) * 256, :] = m.T

    def band_slice(a, f, start, size):
        parts = []
        for k in range(4):
            lo, hi = max(start, k * BAND), min(start + size, (k + 1) * BAND)
            if lo < hi:
                parts.append(g[a, f, pl.ds(pl.multiple_of(band_rows(k) + lo - k * BAND, 64), hi - lo), :])
        return parts[0] if len(parts) == 1 else jnp.concatenate(parts, axis=0)

    def wgrad_chunk(q):
        start, size, _ = CHUNKS[q]
        rhs = jnp.concatenate([band_slice(0, f, start, size) for f in range(NF)], axis=1)
        acc = lax.dot_general(csp[...], rhs, (((1,), (1,)), ((), ())), preferred_element_type=jnp.float32)
        for c in range(2):
            pw[q][c] = acc[c * nz * ROWS:(c + 1) * nz * ROWS].reshape(nz, ROWS, size)
        remote(pw[q].at[1 - core], mb[q], m_s.at[q], m_r.at[q], sib)

    def hops(q, i):
        n = CHUNKS[q][2]
        return n if i == 0 else 7 - n

    def rs_wait(q, i, k):
        wait_for(rp[q].at[i, k], rs_s.at[i, q, k], rs_r.at[i, q, k])

    def rs_send(q, i, k):
        if k >= hops(q, i):
            return
        dist = hops(q, i) - k
        to = lax.rem(z + (dist if i == 0 else nz - dist), nz)
        if k > 0:
            rs_wait(q, i, k - 1)
            mb[q][to] = mb[q][to] + rp[q][i, k - 1]
        remote(mb[q].at[to], rp[q].at[i, k], rs_s.at[i, q, k], rs_r.at[i, q, k],
               zdev(1 if i == 0 else -1))

    def rs_start(q):
        wait_for(mb[q], m_s.at[q], m_r.at[q])
        mb[q][...] = mb[q][...] + pw[q][core]
        rs_send(q, 0, 0)
        rs_send(q, 1, 0)

    def rs_round(q, k):
        rs_send(q, 0, k)
        rs_send(q, 1, k)

    def store(vmem, hbm, sem):
        cp = pltpu.make_async_copy(vmem, hbm, sem)
        cp.start()
        loads[len(loads) + 100] = cp

    def convolved(lhs, rhs, sign):
        prod = jnp.dot(lhs[0:TAPS * CH, :], rhs, preferred_element_type=jnp.float32)
        total = None
        for t in range(TAPS):
            dy, dx = offsets(t)
            term = moved(prod[t * CH:(t + 1) * CH], sign * dy, sign * dx)
            total = term if total is None else total + term
        return total

    def respond(f):
        eye = (lax.broadcasted_iota(jnp.int32, (CH, CH), 0) == lax.broadcasted_iota(jnp.int32, (CH, CH), 1))
        column = jnp.sum(jnp.where(eye, bias_ref[...], 0.0), axis=1, keepdims=True)
        resp[f] = (convolved(ws, g[0, f], 1) + column).astype(jnp.bfloat16)

    def grad_of(f):
        fgrad[f] = convolved(rt, band_slice(1, f, 0, C), -1).astype(jnp.bfloat16)

    own_sends(0)
    for t in range(TAPS):
        loads[t].wait()
    own_piece = send_slices()
    loads["perm"].wait()
    shifted(0)
    events(0, (1, 0), (3, 0), (0, 1))
    shifted(1)
    events(0, (2, 0), (0, 2), (0, 3))
    z_start(own_piece)
    shifted(2)
    events(0, (1, 1), (3, 1))
    shifted(3)
    events(0, (2, 1))
    band(0, 0)
    wgrad_chunk(0)
    own_sends(1)
    z_relay(1)
    rs_start(0)
    band(0, 1)
    wgrad_chunk(1)
    events(1, (1, 0), (3, 0), (0, 1))
    z_relay(2)
    band(0, -1)
    wgrad_chunk(2)
    rs_start(1)
    rs_round(0, 1)
    z_relay(3)
    events(1, (2, 0), (0, 2), (0, 3))
    band(0, 2)
    wgrad_chunk(3)
    rs_start(2)
    rs_round(0, 2)
    rs_round(1, 1)
    events(1, (1, 1), (3, 1), (2, 1))
    z_relay(4)
    rs_start(3)
    rs_round(0, 3)
    respond(0)
    rs_round(2, 1)
    rs_round(1, 2)
    respond(1)
    rs_round(3, 1)
    rs_round(2, 2)
    rs_round(1, 3)
    z_finish()
    for group in range(3):
        turn(group)
    rs_round(3, 2)
    rs_round(2, 3)
    respond(2)
    respond(3)
    store(resp, resp_hbm, osem.at[0])
    rs_round(3, 3)
    for step in BANDS:
        band(1, step)
    for f in range(NF):
        grad_of(f)
    store(fgrad, fgrad_hbm, osem.at[1])

    parts = []
    for q in range(len(CHUNKS)):
        for i in range(2):
            rs_wait(q, i, hops(q, i) - 1)
        parts.append(mb[q][z] + rp[q][0, hops(q, 0) - 1] + rp[q][1, hops(q, 1) - 1])
    final = jnp.concatenate(parts, axis=1)
    for case in range(4):
        @pl.when(y == case)
        def _(case=case):
            where = {(case + step) % 4: k for k, step in enumerate(BANDS)}
            ordered = jnp.concatenate(
                [final[:, where[row] * BAND:(where[row] + 1) * BAND] for row in range(4)], axis=1)
            for t in range(TAPS):
                wgrad[:, t * C:(t + 1) * C] = ordered[t * 5:(t + 1) * 5]
    store(wgrad, wgrad_hbm, osem.at[2])

    for cp in pending:
        cp.wait_send()
    for name, cp in loads.items():
        if isinstance(name, int) and name >= 100:
            cp.wait()


def hand_over(a, b, c, a_out, b_out, c_out, a_v, b_v, c_v, sem_in, sem_out):
    trio = ((a, a_v, a_out), (b, b_v, b_out), (c, c_v, c_out))
    ins = [pltpu.make_async_copy(src, v, sem_in.at[i]) for i, (src, v, _) in enumerate(trio)]
    outs = [pltpu.make_async_copy(v, dst, sem_out.at[i]) for i, (_, v, dst) in enumerate(trio)]
    for cp in ins:
        cp.start()
    for one, two in zip(ins, outs):
        one.wait()
        two.start()
    for cp in outs:
        cp.wait()


def solution(mesh):
    nz = mesh.shape["dp"] // 2
    table = np.zeros((PAD, TAPS * CH), np.float32)
    for c in range(2):
        for k in range(nz):
            for t in range(TAPS):
                for j in range(5):
                    table[c * nz * ROWS + k * ROWS + t * 5 + j, t * CH + k * 10 + c * 5 + j] = 1
    table = table.astype(ml_dtypes.bfloat16)

    bf16, f32 = jnp.bfloat16, jnp.float32
    vmem = pl.BlockSpec(memory_space=pltpu.VMEM)
    hbm = pl.BlockSpec(memory_space=pl.ANY)
    dma = pltpu.SemaphoreType.DMA
    nq = len(CHUNKS)
    outs = ((NF, CH, CELLS), bf16), ((NF, CH, CELLS), bf16), ((5, TAPS * C), f32)
    shapes = tuple(jax.ShapeDtypeStruct(*o) for o in outs)

    def body(frames, weight, bias, cotangent):
        results = pl.pallas_call(
            functools.partial(kernel, nz),
            out_shape=shapes,
            in_specs=[hbm, hbm, vmem, hbm, hbm],
            out_specs=(hbm, hbm, hbm),
            scratch_shapes=[
                pltpu.VMEM((2, NF, C, CELLS), bf16),
                pltpu.VMEM((TAPS * CH, C), bf16),
                pltpu.VMEM((NB, 16, 256), bf16),
                pltpu.VMEM((NB, 6, 3, 16, 256), bf16),
                pltpu.VMEM((PAD, C), bf16),
                pltpu.VMEM((PAD, TAPS * CH), bf16),
                pltpu.VMEM((TAPS * CH, CELLS), bf16),
                pltpu.VMEM((PAD, NF * CELLS), bf16),
                *[pltpu.VMEM(*o) for o in outs],
                *[pltpu.VMEM((2, nz, ROWS, n), f32) for _, n, _ in CHUNKS],
                *[pltpu.VMEM((nz, ROWS, n), f32) for _, n, _ in CHUNKS],
                *[pltpu.VMEM((2, 4, ROWS, n), f32) for _, n, _ in CHUNKS],
                dma((2, NF)), dma((TAPS + 1,)), dma((3,)),
                dma((2, NF, 15)), dma((2, NF, 16)),
                dma((NB,)), dma((NB,)),
                dma((2, 4)), dma((2, 5)),
                dma((2, 5)), dma((2, 5)),
                dma((nq,)), dma((nq,)),
                dma((2, nq, 4)), dma((2, nq, 4)),
            ],
            compiler_params=pltpu.CompilerParams(
                collective_id=0, has_side_effects=True, vmem_limit_bytes=60 * 1024 * 1024),
        )(frames, weight, bias.reshape(1, CH), cotangent, jnp.asarray(table))
        return pl.pallas_call(
            hand_over,
            out_shape=shapes,
            in_specs=[hbm] * 3,
            out_specs=(hbm,) * 3,
            scratch_shapes=[*[pltpu.VMEM(*o) for o in outs], dma((3,)), dma((3,))],
        )(*results)

    return jax.shard_map(
        body,
        mesh=mesh,
        in_specs=(P("dp", "blk", None), P("blk", None), P("blk"), P("dp", "blk", None)),
        out_specs=(P("dp", "blk", None), P("dp", "blk", None), P(("blk", "dp"), None)),
        check_vma=False,
    )
```

time: 335 us -> 66.2 us (0.20)
  the two profiles are of different devices: /device:TPU:1 before, /device:TPU:8 now
where the time goes in v2:
time: 66.2 us; the launch traced here: 66 us
  Pallas kernels  65.4 us (99%)
    pallas_call x1, Pallas kernels, body(): pl.pallas_call(functools.partial(kernel, nz), out_shape=shapes, in_specs=...  63.5 us
    pallas_call x1, Pallas kernels, body(): pl.pallas_call(hand_over, out_shape=shapes, in_specs=[hbm] * 3, out_specs...  1.94 us

profile of v2, /device:TPU:8, one launch (start us, length us, event | category | flops | bytes accessed | tf_op | source)
XLA Modules:
  0.0 66.0 jit_solution(13152836793104299492)
XLA Ops:
  0.6 63.5 %shard_map.76 = (bf16[4,80,256]{2,1,0:T(8,128)(2,1)}, bf16[4,80,256]{2,1,0:T(8,128)(2,1)}, f32[5,11520]{1,0:T(8,128)}) custom-call(bf16[4,80,256]{2,1,0:T(8,128)(2,1)} %frames_hbm.1, bf16[80,11520]{1,0:T(8,128)(2,1)} %weight_hbm.1, f32[1,80]{1,0:T(1,128)} %bitcast.1, bf16[4,80,256]{2,1,0:T(8,128)(2,1)} %cot_hbm.1, bf16[768,720]{1,0:T(8,128)(2,1)} %constant.2.clone.perm_hbm), custom_call_target="tpu_custom_call" | custom-call | tf_op jit(solution)/shard_map/pallas_call | solution.py:425
  64.1 1.9 %shard_map.77 = (bf16[4,80,256]{2,1,0:T(8,128)(2,1)}, bf16[4,80,256]{2,1,0:T(8,128)(2,1)}, f32[5,11520]{1,0:T(8,128)}) custom-call(bf16[4,80,256]{2,1,0:T(8,128)(2,1)} %get-tuple-element.6.a, bf16[4,80,256]{2,1,0:T(8,128)(2,1)} %get-tuple-element.7.b, f32[5,11520]{1,0:T(8,128)} %get-tuple-element.8.c), custom_call_target="tpu_custom_call" | custom-call | tf_op jit(solution)/shard_map/pallas_call | solution.py:454

commit v3 on v2

v3 whole, which is shorter than its diff:
```python
import functools

import jax
import jax.numpy as jnp
import ml_dtypes
import numpy as np
from jax import lax
from jax.experimental import pallas as pl
from jax.experimental.pallas import tpu as pltpu
from jax.sharding import PartitionSpec as P

MESH = pl.DeviceIdType.MESH
CH = 80
NB = 16
C = CH * NB
TAPS = 9
CELLS = 256
NF = 4
PAD = 768
ROWS = 48

TREES = [(True, 1), (True, -1), (False, 1), (False, -1)]
STEPS = [0, 1, -1, 2]
ARRIVAL = [(0, 0), (1, 0), (2, 0), (0, 1), (0, 2), (3, 0), (0, 3), (1, 1), (1, 2), (2, 1), (2, 2),
           (3, 1), (3, 2), (1, 3), (2, 3), (3, 3)]
CHUNKS = [(0, 384, 4), (384, 384, 3), (768, 256, 3), (1024, 256, 4)]

ORDER = [
    ('wx',), ('own', 0, False), ('own', 0, True), ('block', 0, 1, 0, 1), ('wy',), ('block', 0, 1, 1, 0),
    ('block', 0, 0, 1, 0), ('block', 0, 0, 0, 1), ('block', 0, 3, 3, 0), ('shift', 1), ('block', 0, 0, 3, 0),
    ('block', 0, 2, 3, 0), ('block', 0, 1, 3, 0), ('block', 0, 2, 0, 1), ('shift', 2), ('block', 0, 3, 0, 1),
    ('block', 0, 1, 2, 0), ('block', 0, 3, 0, 3), ('block', 0, 3, 1, 0), ('block', 0, 2, 1, 0), ('own', 1, False),
    ('wz',), ('block', 0, 1, 0, 3), ('block', 0, 2, 0, 3), ('shift', 3), ('own', 1, True), ('shift', 0),
    ('block', 0, 3, 3, 1), ('block', 0, 0, 0, 3), ('block', 0, 0, 1, 3), ('block', 0, 0, 0, 2), ('chunk', 0),
    ('block', 0, 1, 1, 1), ('hop', 1, 1, 0), ('hop', 0, 1, 0), ('block', 0, 1, 2, 3), ('block', 0, 1, 3, 1),
    ('block', 0, 1, 0, 2), ('block', 0, 1, 1, 3), ('hop', 1, 1, 1), ('hop', 0, 1, 1), ('block', 0, 2, 1, 1),
    ('block', 0, 3, 1, 1), ('block', 0, 1, 3, 3), ('block', 0, 2, 3, 3), ('block', 1, 1, 1, 0),
    ('block', 0, 0, 2, 0), ('block', 0, 0, 1, 1), ('block', 0, 3, 0, 2), ('block', 0, 2, 3, 1),
    ('block', 0, 3, 1, 3), ('block', 0, 2, 0, 2), ('block', 0, 2, 2, 0), ('block', 0, 0, 3, 3),
    ('block', 0, 0, 3, 1), ('merge', 0), ('block', 0, 2, 1, 3), ('block', 0, 3, 2, 0), ('chunk', 1),
    ('block', 1, 3, 1, 0), ('hop', 1, 2, 0), ('hop', 0, 2, 0), ('block', 0, 2, 1, 2), ('block', 0, 3, 1, 2),
    ('block', 1, 2, 1, 0), ('block', 0, 3, 3, 2), ('block', 0, 3, 3, 3), ('hop', 1, 2, 1), ('block', 0, 1, 1, 2),
    ('block', 0, 1, 2, 1), ('merge', 1), ('block', 0, 2, 3, 2), ('block', 0, 2, 2, 1), ('hop', 0, 2, 1),
    ('block', 0, 0, 2, 1), ('sum', 0, 0, 1), ('sum', 0, 1, 1), ('block', 0, 0, 2, 3), ('block', 1, 0, 3, 0),
    ('block', 0, 3, 2, 1), ('block', 1, 3, 0, 1), ('block', 1, 0, 1, 0), ('chunk', 2), ('block', 1, 1, 2, 0),
    ('block', 1, 3, 3, 0), ('block', 0, 1, 2, 2), ('block', 0, 0, 1, 2), ('block', 0, 0, 3, 2),
    ('block', 0, 3, 2, 3), ('block', 0, 1, 3, 2), ('block', 1, 2, 2, 0), ('block', 1, 3, 2, 0),
    ('block', 1, 2, 3, 0), ('merge', 2), ('block', 1, 2, 0, 1), ('block', 0, 3, 2, 2), ('block', 0, 2, 2, 2),
    ('block', 0, 2, 2, 3), ('block', 1, 1, 1, 1), ('block', 0, 0, 2, 2), ('chunk', 3), ('block', 1, 0, 2, 0),
    ('sum', 1, 1, 1), ('sum', 1, 0, 1), ('block', 1, 1, 3, 0), ('block', 1, 2, 1, 1), ('resp', 3),
    ('hop', 1, 3, 1), ('block', 1, 3, 1, 1), ('block', 1, 0, 3, 1), ('block', 1, 2, 2, 1), ('block', 1, 1, 2, 1),
    ('block', 1, 3, 3, 1), ('merge', 3), ('block', 1, 1, 0, 1), ('hop', 0, 3, 0), ('block', 1, 0, 0, 1),
    ('block', 1, 0, 1, 1), ('block', 1, 0, 2, 1), ('block', 1, 3, 2, 1), ('block', 1, 1, 3, 1),
    ('block', 1, 2, 3, 1), ('sum', 0, 0, 2), ('hop', 0, 3, 1), ('sum', 2, 1, 1), ('sum', 1, 1, 2),
    ('sum', 3, 0, 1), ('sum', 0, 1, 2), ('sum', 2, 0, 1), ('hop', 1, 3, 0), ('sum', 1, 0, 2), ('hop', 0, 4, 0),
    ('hop', 1, 4, 1), ('sum', 2, 1, 2), ('sum', 3, 1, 1), ('sum', 1, 1, 3), ('sum', 3, 0, 2), ('turn',),
    ('sum', 0, 0, 3), ('sum', 2, 0, 2), ('grad', 1), ('sum', 2, 1, 3), ('grad', 2), ('sum', 3, 1, 2),
    ('sum', 3, 0, 3), ('grad', 3), ('resp', 1), ('resp', 2), ('resp', 0), ('grad', 0),
]


def offsets(tap):
    return tap // 3 - 1, tap % 3 - 1


def moved(v, dy, dx):
    if dy == 0 and dx == 0:
        return v
    cell = lax.broadcasted_iota(jnp.int32, (1, CELLS), 1)
    h = lax.shift_right_logical(cell, 4) + dy
    w = lax.bitwise_and(cell, 15) + dx
    keep = (h >= 0) & (h < 16) & (w >= 0) & (w < 16)
    rolled = pltpu.roll(v, (-(dy * 16 + dx)) % CELLS, axis=1)
    return jnp.where(keep, rolled, jnp.zeros_like(rolled))


def kernel(nz, frames_hbm, weight_hbm, bias_ref, cot_hbm, perm_hbm,
           resp_hbm, fgrad_hbm, wgrad_hbm,
           g, ws, pb, xb, r, rt, perm, cst, csp, resp, fgrad, wgrad, mixed,
           pw0, pw1, pw2, pw3, mb0, mb1, mb2, mb3, rp0, rp1, rp2, rp3,
           lsem, osem, ag_s, ag_r, w_s, w_r, z_s, z_r, d_s, d_r,
           m_s, m_r, rs_s, rs_r):
    pw, mb, rp = (pw0, pw1, pw2, pw3), (mb0, mb1, mb2, mb3), (rp0, rp1, rp2, rp3)
    dp = lax.axis_index("dp")
    blk = lax.axis_index("blk")
    z, core = dp // 2, lax.rem(dp, 2)
    y, x = blk // 4, lax.rem(blk, 4)
    sib = (z * 2 + 1 - core, blk)

    def plane(b):
        return (dp, b)

    def across(sx, sy):
        return lax.rem(y + sy, 4) * 4 + lax.rem(x + sx, 4)

    def zdev(step):
        return (lax.rem(z + step + nz, nz) * 2 + core, blk)

    own_rows = pl.ds(pl.multiple_of(blk * CH, 16), CH)

    loads = {}

    def load(name, src, dst, sem):
        loads[name] = pltpu.make_async_copy(src, dst, sem)
        loads[name].start()

    load("frames", frames_hbm, g.at[0, :, own_rows, :], lsem.at[0])
    load("cot", cot_hbm, g.at[1, :, own_rows, :], lsem.at[1])
    for t in range(TAPS):
        load(t, weight_hbm.at[:, pl.ds(t * C, C)], ws.at[pl.ds(t * CH, CH), :], lsem.at[2])
    load("perm", perm_hbm, perm, lsem.at[3])

    barrier = pltpu.get_barrier_semaphore()
    partners = [plane(across(k, 0)) for k in (1, 2, 3)] + [plane(across(0, k)) for k in (1, 2, 3)]
    for dev in (*partners, sib, zdev(1), zdev(-1)):
        pl.semaphore_signal(barrier, inc=1, device_id=dev, device_id_type=MESH)
    loads["frames"].wait()
    loads["cot"].wait()
    pl.semaphore_wait(barrier, 9)

    def remote(src, dst, ssem, rsem, dev):
        pltpu.make_async_remote_copy(
            src_ref=src, dst_ref=dst, send_sem=ssem, recv_sem=rsem,
            device_id=dev, device_id_type=MESH).start()

    def wait_for(ref, ssem, rsem):
        pltpu.make_async_remote_copy(
            src_ref=ref, dst_ref=ref, send_sem=ssem, recv_sem=rsem,
            device_id=sib, device_id_type=MESH).wait_recv()

    def all_sent(ref, ssem, rsem):
        pltpu.make_async_remote_copy(
            src_ref=ref, dst_ref=ref, send_sem=ssem, recv_sem=rsem,
            device_id=sib, device_id_type=MESH).wait_send()

    def at(tree, step_a, step_b):
        first_x, _ = TREES[tree]
        sx, sy = (step_a, step_b) if first_x else (step_b, step_a)
        return lax.rem(y + sy + 4, 4) * 4 + lax.rem(x + sx + 4, 4)

    def block(a, f, ra, rb):
        sgn = TREES[f][1]
        src = at(f, -sgn * (ra if ra < 3 else -1), -sgn * (rb if rb < 3 else -1))
        return g.at[a, f, pl.ds(pl.multiple_of(src * CH, 16), CH), :]

    def ag_sem(a, f, ra, rb):
        if a == 1 and rb > 1 or a == 1 and (ra, rb) == (0, 3):
            return ag_r.at[1, f, 0]
        return ag_r.at[a, f, ra * 4 + rb]

    def push(a, f, ra, rb, along_a, forward):
        sgn = TREES[f][1]
        step = sgn if forward else -sgn
        dev = at(f, step, 0) if along_a else at(f, 0, step)
        if along_a:
            there = (ra + 1 if forward else 3, rb)
        else:
            there = (ra, rb + 1 if forward else 3)
        ref = block(a, f, ra, rb)
        remote(ref, ref, ag_s.at[a], ag_sem(a, f, *there), plane(dev))

    def block_task(a, f, ra, rb):
        wait_for(block(a, f, ra, rb), ag_s.at[a], ag_sem(a, f, ra, rb))
        if rb == 0:
            if ra == 1:
                push(a, f, ra, rb, True, True)
            push(a, f, ra, rb, False, True)
            push(a, f, ra, rb, False, False)
        elif rb == 1:
            push(a, f, ra, rb, False, True)

    def own_sends(a, along_x):
        for forward in (True, False):
            for f in range(NF):
                push(a, f, 0, 0, TREES[f][0] == along_x, forward)

    def shifted(f):
        if "perm" in loads:
            loads.pop("perm").wait()
        cot = g[1, f, own_rows, :].astype(jnp.float32)
        for t in range(TAPS):
            dy, dx = offsets(t)
            cst[t * CH:(t + 1) * CH, :] = moved(cot, -dy, -dx).astype(jnp.bfloat16)
        csp[:, f * CELLS:(f + 1) * CELLS] = jnp.dot(
            perm[...], cst[...], preferred_element_type=jnp.float32).astype(jnp.bfloat16)

    def piece_of(zz, cc):
        d = zz * 2 + cc
        return d // 3, lax.rem(d, 3)

    my_row, my_group = piece_of(z, core)
    row_start = pl.multiple_of(jnp.minimum(my_row, 4) * 16, 16)

    def pack(group):
        for b in range(NB):
            parts = []
            for t in range(TAPS):
                lo, hi = max(t * CH, group * 256), min((t + 1) * CH, (group + 1) * 256)
                if lo < hi:
                    parts.append(ws[pl.ds(pl.multiple_of(t * CH + row_start, 16), 16),
                                    b * CH + lo - t * CH:b * CH + hi - t * CH])
            if group == 2:
                parts.append(jnp.zeros((16, PAD - TAPS * CH), jnp.bfloat16))
            pb[b % 4, b // 4] = jnp.concatenate(parts, axis=1)

    def slices_along_x():
        pltpu.make_async_copy(ws, ws, lsem.at[2]).wait()
        for group in range(3):
            @pl.when(my_group == group)
            def _(group=group):
                pack(group)
        load("x", pb.at[x], xb.at[x], lsem.at[4])
        for k in (1, 3, 2):
            remote(pb.at[lax.rem(x + k, 4)], xb.at[x], w_s.at[0], w_r.at[0], plane(across(k, 0)))

    def slices_along_y():
        loads["x"].wait()
        wait_for(xb.at[pl.ds(0, 3)], w_s.at[0], w_r.at[0])
        here = r.at[pl.ds(y * 4, 4), my_row, my_group]
        load("y", xb.at[:, y], here, lsem.at[5])
        for k in (1, 3, 2):
            remote(xb.at[:, lax.rem(y + k, 4)], here, w_s.at[1], w_r.at[1], plane(across(0, k)))

    def z_piece(i, k, h, cc):
        zz = lax.rem(z + (-k if i == 0 else k) + nz, nz)
        row, group = piece_of(zz, cc)
        return r.at[pl.ds(h * 8, 8), row, group]

    def z_push(i, k, h):
        ref = z_piece(i, k, h, core)
        remote(ref, ref, z_s.at[0], z_r.at[i, k, h], zdev(1 if i == 0 else -1))

    def to_sibling(i, k, h):
        ref = z_piece(i, k, h, core)
        remote(ref, ref, d_s.at[0], d_r.at[0], sib)

    def slices_along_z():
        loads["y"].wait()
        wait_for(xb.at[pl.ds(0, 3)], w_s.at[1], w_r.at[1])
        for h in range(2):
            z_push(0, 0, h)
            z_push(1, 0, h)
        for h in range(2):
            to_sibling(0, 0, h)

    def z_task(i, k, h):
        wait_for(z_piece(i, k, h, core), z_s.at[0], z_r.at[i, k - 1, h])
        if k < 3 or (k == 3 and h == i):
            z_push(i, k, h)
        to_sibling(i, k, h)

    def slices_done():
        wait_for(r.at[:, 0:4, 0:2], d_s.at[0], d_r.at[0])
        for group in range(3):
            turn(group)

    def turn(group):
        m = r[:, 0:5, group].reshape(C, 256)
        rt[group * 256:(group + 1) * 256, :] = m.T

    def arrived_rows(f, start, size):
        parts = []
        for n, (kx, ky) in enumerate(ARRIVAL):
            lo, hi = max(start, n * CH), min(start + size, (n + 1) * CH)
            if lo < hi:
                src = lax.rem(y + STEPS[ky] + 4, 4) * 4 + lax.rem(x + STEPS[kx] + 4, 4)
                parts.append(g[0, f, pl.ds(pl.multiple_of(src * CH + lo - n * CH, 16), hi - lo), :])
        return jnp.concatenate(parts, axis=0)

    def wgrad_chunk(q):
        start, size, _ = CHUNKS[q]
        rhs = jnp.concatenate([arrived_rows(f, start, size) for f in range(NF)], axis=1)
        acc = lax.dot_general(csp[...], rhs, (((1,), (1,)), ((), ())), preferred_element_type=jnp.float32)
        for c in range(2):
            pw[q][c] = acc[c * nz * ROWS:(c + 1) * nz * ROWS].reshape(nz, ROWS, size)
        remote(pw[q].at[1 - core], mb[q], m_s.at[q], m_r.at[q], sib)

    def hops(q, i):
        n = CHUNKS[q][2]
        return n if i == 0 else 7 - n

    def rs_wait(q, i, k):
        wait_for(rp[q].at[i, k], rs_s.at[q], rs_r.at[i, q, k])

    def rs_send(q, i, k):
        if k >= hops(q, i):
            return
        dist = hops(q, i) - k
        to = lax.rem(z + (dist if i == 0 else nz - dist), nz)
        if k > 0:
            rs_wait(q, i, k - 1)
            mb[q][to] = mb[q][to] + rp[q][i, k - 1]
        remote(mb[q].at[to], rp[q].at[i, k], rs_s.at[q], rs_r.at[i, q, k],
               zdev(1 if i == 0 else -1))

    def rs_start(q):
        wait_for(mb[q], m_s.at[q], m_r.at[q])
        mb[q][...] = mb[q][...] + pw[q][core]
        rs_send(q, 0, 0)
        rs_send(q, 1, 0)

    def store(vmem, hbm, sem):
        cp = pltpu.make_async_copy(vmem, hbm, sem)
        cp.start()
        loads[len(loads) + 100] = cp

    def convolved(lhs, rhs, sign):
        prod = jnp.dot(lhs[0:TAPS * CH, :], rhs, preferred_element_type=jnp.float32)
        total = None
        for t in range(TAPS):
            dy, dx = offsets(t)
            term = moved(prod[t * CH:(t + 1) * CH], sign * dy, sign * dx)
            total = term if total is None else total + term
        return total

    def respond(f):
        eye = (lax.broadcasted_iota(jnp.int32, (CH, CH), 0) == lax.broadcasted_iota(jnp.int32, (CH, CH), 1))
        column = jnp.sum(jnp.where(eye, bias_ref[...], 0.0), axis=1, keepdims=True)
        resp[f] = (convolved(ws, g[0, f], 1) + column).astype(jnp.bfloat16)

    def grad_of(f):
        wait_for(g.at[1, f, pl.ds(0, 8 * CH), :], ag_s.at[1], ag_r.at[1, f, 0])
        fgrad[f] = convolved(rt, g[1, f], -1).astype(jnp.bfloat16)

    tasks = {
        "own": own_sends, "block": block_task, "shift": shifted, "chunk": wgrad_chunk,
        "merge": rs_start, "sum": rs_send, "resp": respond, "grad": grad_of,
        "wx": slices_along_x, "wy": slices_along_y, "wz": slices_along_z,
        "hop": z_task, "turn": slices_done,
    }
    for name, *rest in ORDER:
        tasks[name](*rest)
    store(resp, resp_hbm, osem.at[0])
    store(fgrad, fgrad_hbm, osem.at[1])

    parts = []
    for q in range(len(CHUNKS)):
        for i in range(2):
            rs_wait(q, i, hops(q, i) - 1)
        parts.append(mb[q][z] + rp[q][0, hops(q, 0) - 1] + rp[q][1, hops(q, 1) - 1])
    final = jnp.concatenate(parts, axis=1)
    place = {block: n for n, block in enumerate(ARRIVAL)}
    for case in range(4):
        where = {(case + step) % 4: k for k, step in enumerate(STEPS)}

        @pl.when(x == case)
        def _(where=where):
            pieces = [place[where[col], ky] for ky in range(4) for col in range(4)]
            mixed[...] = jnp.concatenate([final[:, n * CH:(n + 1) * CH] for n in pieces], axis=1)

    for case in range(4):
        where = {(case + step) % 4: k for k, step in enumerate(STEPS)}

        @pl.when(y == case)
        def _(where=where):
            bands = [where[row] * 4 * CH for row in range(4)]
            ordered = jnp.concatenate([mixed[:, n:n + 4 * CH] for n in bands], axis=1)
            for t in range(TAPS):
                wgrad[:, t * C:(t + 1) * C] = ordered[t * 5:(t + 1) * 5]
    store(wgrad, wgrad_hbm, osem.at[2])

    for a in range(2):
        all_sent(g.at[a, :, pl.ds(0, 15 * CH), :], ag_s.at[a], ag_r.at[a, 0, 1])
        all_sent(xb.at[pl.ds(0, 3)], w_s.at[a], w_r.at[a])
    all_sent(r.at[pl.ds(0, 14), 0:4, 0:2], z_s.at[0], z_r.at[0, 0, 0])
    all_sent(r.at[:, 0:4, 0:2], d_s.at[0], d_r.at[0])
    for q in range(len(CHUNKS)):
        all_sent(mb[q], m_s.at[q], m_r.at[q])
        all_sent(mb[q].at[pl.ds(0, nz - 1)], rs_s.at[q], rs_r.at[0, q, 0])
    for name, cp in loads.items():
        if isinstance(name, int) and name >= 100:
            cp.wait()


def hand_over(a, b, c, a_out, b_out, c_out, a_v, b_v, c_v, sem_in, sem_out):
    trio = ((a, a_v, a_out), (b, b_v, b_out), (c, c_v, c_out))
    ins = [pltpu.make_async_copy(src, v, sem_in.at[i]) for i, (src, v, _) in enumerate(trio)]
    outs = [pltpu.make_async_copy(v, dst, sem_out.at[i]) for i, (_, v, dst) in enumerate(trio)]
    for cp in ins:
        cp.start()
    for one, two in zip(ins, outs):
        one.wait()
        two.start()
    for cp in outs:
        cp.wait()


def solution(mesh):
    nz = mesh.shape["dp"] // 2
    table = np.zeros((PAD, TAPS * CH), np.float32)
    for c in range(2):
        for k in range(nz):
            for t in range(TAPS):
                for j in range(5):
                    table[c * nz * ROWS + k * ROWS + t * 5 + j, t * CH + k * 10 + c * 5 + j] = 1
    table = table.astype(ml_dtypes.bfloat16)

    bf16, f32 = jnp.bfloat16, jnp.float32
    vmem = pl.BlockSpec(memory_space=pltpu.VMEM)
    hbm = pl.BlockSpec(memory_space=pl.ANY)
    dma = pltpu.SemaphoreType.DMA
    nq = len(CHUNKS)
    outs = ((NF, CH, CELLS), bf16), ((NF, CH, CELLS), bf16), ((5, TAPS * C), f32)
    shapes = tuple(jax.ShapeDtypeStruct(*o) for o in outs)

    def body(frames, weight, bias, cotangent):
        results = pl.pallas_call(
            functools.partial(kernel, nz),
            out_shape=shapes,
            in_specs=[hbm, hbm, vmem, hbm, hbm],
            out_specs=(hbm, hbm, hbm),
            scratch_shapes=[
                pltpu.VMEM((2, NF, C, CELLS), bf16),
                pltpu.VMEM((TAPS * CH, C), bf16),
                pltpu.VMEM((4, 4, 16, 256), bf16),
                pltpu.VMEM((4, 4, 16, 256), bf16),
                pltpu.VMEM((NB, 6, 3, 16, 256), bf16),
                pltpu.VMEM((PAD, C), bf16),
                pltpu.VMEM((PAD, TAPS * CH), bf16),
                pltpu.VMEM((TAPS * CH, CELLS), bf16),
                pltpu.VMEM((PAD, NF * CELLS), bf16),
                *[pltpu.VMEM(*o) for o in outs],
                pltpu.VMEM((ROWS, C), f32),
                *[pltpu.VMEM((2, nz, ROWS, n), f32) for _, n, _ in CHUNKS],
                *[pltpu.VMEM((nz, ROWS, n), f32) for _, n, _ in CHUNKS],
                *[pltpu.VMEM((2, 4, ROWS, n), f32) for _, n, _ in CHUNKS],
                dma((6,)), dma((3,)),
                dma((2,)), dma((2, NF, 16)),
                dma((2,)), dma((2,)),
                dma((1,)), dma((2, 4, 2)),
                dma((1,)), dma((1,)),
                dma((nq,)), dma((nq,)),
                dma((nq,)), dma((2, nq, 4)),
            ],
            compiler_params=pltpu.CompilerParams(
                collective_id=0, has_side_effects=True, vmem_limit_bytes=60 * 1024 * 1024),
        )(frames, weight, bias.reshape(1, CH), cotangent, jnp.asarray(table))
        return pl.pallas_call(
            hand_over,
            out_shape=shapes,
            in_specs=[hbm] * 3,
            out_specs=(hbm,) * 3,
            scratch_shapes=[*[pltpu.VMEM(*o) for o in outs], dma((3,)), dma((3,))],
        )(*results)

    return jax.shard_map(
        body,
        mesh=mesh,
        in_specs=(P("dp", "blk", None), P("blk", None), P("blk"), P("dp", "blk", None)),
        out_specs=(P("dp", "blk", None), P("dp", "blk", None), P(("blk", "dp"), None)),
        check_vma=False,
    )
```

time: 66.2 us -> 57.5 us (0.87)
  the two profiles are of different devices: /device:TPU:8 before, /device:TPU:1 now
where the time goes in v3:
time: 57.5 us; the launch traced here: 57.4 us
  Pallas kernels  56.7 us (99%)
  between operations  0.64 us (1%)
    pallas_call x1, Pallas kernels, body(): pl.pallas_call(functools.partial(kernel, nz), out_shape=shapes, in_specs=...  54.8 us
    pallas_call x1, Pallas kernels, body(): pl.pallas_call(hand_over, out_shape=shapes, in_specs=[hbm] * 3, out_specs...  1.94 us

profile of v3, /device:TPU:1, one launch (start us, length us, event | category | flops | bytes accessed | tf_op | source)
XLA Modules:
  0.0 57.4 jit_solution(5095656652438387754)
XLA Ops:
  0.6 54.8 %shard_map.76 = (bf16[4,80,256]{2,1,0:T(8,128)(2,1)}, bf16[4,80,256]{2,1,0:T(8,128)(2,1)}, f32[5,11520]{1,0:T(8,128)}) custom-call(bf16[4,80,256]{2,1,0:T(8,128)(2,1)} %frames_hbm.1, bf16[80,11520]{1,0:T(8,128)(2,1)} %weight_hbm.1, f32[1,80]{1,0:T(1,128)} %bitcast.1, bf16[4,80,256]{2,1,0:T(8,128)(2,1)} %cot_hbm.1, bf16[768,720]{1,0:T(8,128)(2,1)} %constant.2.clone.perm_hbm), custom_call_target="tpu_custom_call" | custom-call | tf_op jit(solution)/shard_map/pallas_call | solution.py:407
  55.4 1.9 %shard_map.77 = (bf16[4,80,256]{2,1,0:T(8,128)(2,1)}, bf16[4,80,256]{2,1,0:T(8,128)(2,1)}, f32[5,11520]{1,0:T(8,128)}) custom-call(bf16[4,80,256]{2,1,0:T(8,128)(2,1)} %get-tuple-element.6.a, bf16[4,80,256]{2,1,0:T(8,128)(2,1)} %get-tuple-element.7.b, f32[5,11520]{1,0:T(8,128)} %get-tuple-element.8.c), custom_call_target="tpu_custom_call" | custom-call | tf_op jit(solution)/shard_map/pallas_call | solution.py:438
